TPU v7x, 32 devices: a whole 2x2x4 slice. The times are simulated.
32 devices in a mesh: aux: 4 (over y, x), blk: 8 (over z, core).
Axes of the slice: x: 2, y: 2, z: 4, core: 2. Of those that a mesh axis runs over, the one named last changes fastest.
Arguments:
- three_center: bfloat16 [384, 4, 128, 128], P(('aux', 'blk')), may hold values from -6 to 6
- slot_block: int32 [384], P(('aux', 'blk')), may hold values from 0 to 47
- slot_aux: int32 [384], P(('aux', 'blk')), may hold values from 0 to 1
- live_slots: int32 [32], P(('aux', 'blk')), may hold values from 1 to 12, as said below
- vir_coef: bfloat16 [6144, 256], replicated, may hold values from -0.00478416 to 0.00478416
- eps_occ: float32 [4000], replicated, may hold values from -1.5 to -0.3
- eps_vir: float32 [256], replicated, may hold values from 0.2 to 3
- occ_index: int32 [4], replicated, may hold values from 0 to 3999, as said below
Outputs:
- amplitudes: float32 [4, 256, 4, 256], P('aux', 'blk')
- pair_energy: float32 [4, 4], P('aux')
Inputs may be any that keep to these rules, and one draw needn't show every extreme that they name: The slots in use on a device are its first live_slots ones; the others hold data that is not used. Some device holds exactly 12 slots in use in every draw. `occ_index`: the indices are distinct; the first and the last occupied orbital of the system are in every batch.
All inputs are finite; a program needn't handle non-finite values.
Results may differ from a plain program's by a relative error of at most 0.0035.
Values may be sent and summed in bfloat16 or wider, within the bound.
A program may use at most 64 MiB of HBM per device.

v0:
```python
import jax
import jax.numpy as jnp
from jax import lax
from jax.sharding import PartitionSpec as P

AUX_BLOCKS_DEV = 2


def body(three_center, slot_block, slot_aux, live_slots, vir_coef, eps_occ, eps_vir, occ_index):
    blk_count = lax.axis_size("blk")
    occ_row = lax.axis_index("aux")
    slot_count = three_center.shape[0]
    occ_count = three_center.shape[1]
    ao_span = three_center.shape[3]
    vir_count = vir_coef.shape[1]
    coef_blocks = vir_coef.reshape(vir_coef.shape[0] // ao_span, ao_span, vir_count)
    coefficients = jnp.take(coef_blocks, slot_block, axis=0)
    products = jnp.einsum(
        "soqn,snv->soqv", three_center, coefficients, preferred_element_type=jnp.float32
    )
    keep = (jnp.arange(slot_count) < live_slots[0]).astype(jnp.float32)
    select = (slot_aux[:, None] == jnp.arange(AUX_BLOCKS_DEV)[None, :]).astype(jnp.float32)
    select = select * keep[:, None]
    local_rows = jnp.einsum("sk,soqv->kqov", select, products).astype(jnp.bfloat16)
    halfed = lax.all_gather(local_rows, "aux", axis=0, tiled=True)
    own_rows = lax.dynamic_index_in_dim(halfed, occ_row, 2, keepdims=False)
    rows_dev = vir_count // blk_count
    mixed = lax.dot_general(
        halfed, own_rows, (((0, 1), (0, 1)), ((), ())), preferred_element_type=jnp.float32
    )
    summed = lax.psum_scatter(
        jnp.stack(
            [
                lax.dot_general(
                    own_rows,
                    halfed,
                    (((0, 1), (0, 1)), ((), ())),
                    preferred_element_type=jnp.float32,
                ),
                jnp.transpose(mixed, (1, 0, 2)),
            ],
            axis=1,
        ),
        "blk",
        scatter_dimension=0,
        tiled=True,
    )
    direct = summed[:, 0]
    crossed = summed[:, 1]
    first_vir = lax.axis_index("blk") * rows_dev
    occ_levels = jnp.take(eps_occ, occ_index)
    own_level = jnp.sum(jnp.where(jnp.arange(occ_count) == occ_row, occ_levels, 0.0))
    vir_levels = lax.dynamic_slice_in_dim(eps_vir, first_vir, rows_dev, 0)
    denominator = (
        own_level + occ_levels[None, :, None] - vir_levels[:, None, None] - eps_vir[None, None, :]
    )
    amplitudes = (direct / denominator)[None]
    pair_part = jnp.sum(direct * (2.0 * direct - crossed) / denominator, axis=(0, 2))
    pair_energy = lax.psum(pair_part, "blk")[None]
    return (amplitudes, pair_energy)


def solution(mesh):
    in_specs = (
        P(("aux", "blk"), None, None, None),
        P(("aux", "blk")),
        P(("aux", "blk")),
        P(("aux", "blk")),
        P(),
        P(),
        P(),
        P(),
    )
    out_specs = (P("aux", "blk", None, None), P("aux", None))
    return jax.shard_map(body, mesh=mesh, in_specs=in_specs, out_specs=out_specs, check_vma=False)
```

profile of v0, /device:TPU:0, one launch (start us, length us, event | category | flops | bytes accessed | tf_op | source)
XLA Modules:
  0.0 131.5 jit_solution(10336060481008152967)
XLA Ops:
  7.2 0.0 copy-start
  7.2 0.0 all-gather.2.cloned.1.call-start
  7.2 0.8 compare_select_fusion.1
  8.0 0.8 compare_and_fusion
  8.8 0.3 copy-done
  9.1 1.5 %gather_fusion = bf16[12,128,256]{2,1,0:T(8,128)(2,1)} fusion(bf16[48,128,256]{2,1,0:T(8,128)(2,1)S(1)} %bitcast.68, s32[1024]{0:T(1024)S(1)} %pad_clamp_fusion.1), kind=kCustom, calls=%fused_computation | custom fusion | bytes 1572912 | tf_op jit(solution)/shard_map/jit(_take)/gather | solution.py:17
  10.6 4.8 %convolution_bitcast_fusion = bf16[12,4,128,256]{2,3,1,0:T(8,128)(2,1)} fusion(bf16[12,4,128,128]{3,2,1,0:T(8,128)(2,1)} %param.8, bf16[12,128,256]{2,1,0:T(8,128)(2,1)} %gather_fusion, pred[12]{0:T(512)(128)(4,1)S(1)} %compare_and_fusion), kind=kOutput, calls=%fused_computation.2 | convolution fusion | flops 403046400 | bytes 5505036 | tf_op jit(solution)/shard_map/soqn,snv->soqv/dot_general | solution.py:18
  15.4 0.0 copy-start.4
  15.4 7.7 %copy.28 = bf16[12,4,128,256]{3,0,2,1:T(8,128)(2,1)} copy(bf16[12,4,128,256]{2,3,1,0:T(8,128)(2,1)} %convolution_bitcast_fusion) | data formatting | bytes 6291456 | tf_op jit(solution)/shard_map/soqn,snv->soqv/dot_general | solution.py:18
  23.7 0.0 copy-done.4
  23.7 2.9 %fusion = bf16[2,128,4,256]{3,0,1,2:T(2,128)(2,1)S(1)} fusion(bf16[12,4,128,256]{3,0,2,1:T(8,128)(2,1)} %copy.28, bf16[12]{0:T(256)(128)(2,1)S(1)} %compare_convert_fusion, s32[12]{0:T(128)S(1)} %copy-done.4), kind=kOutput, calls=%fused_computation.7 | convolution fusion | flops 6291504 | bytes 3670088 | tf_op jit(solution)/shard_map/sk,soqv->kqov/dot_general | solution.py:24
  26.6 0.9 copy.29
  27.5 0.0 all-gather.2.cloned.1.call-update
  27.5 0.0 reduce-scatter.2.cloned.1.call-start
  27.6 38.0 %all-gather.2.cloned.1.call-done = bf16[8,128,4,256]{3,1,2,0:T(8,128)(2,1)} async-done(((bf16[2,128,4,256]{3,1,2,0:T(8,128)(2,1)}), bf16[8,128,4,256]{3,1,2,0:T(8,128)(2,1)}) %all-gather.2.cloned.1.call-update) | async-done | bytes 2097168 | tf_op jit(solution)/shard_map/all_gather | solution.py:25
  65.6 0.0 copy-start.5
  65.6 2.6 %convolution_bitcast_fusion.2 = f32[256,1,4,256]{3,0,2,1:T(8,128)S(1)} fusion(bf16[8,128,4,256]{3,1,2,0:T(8,128)(2,1)} %all-gather.2.cloned.1.call-done, s32[]{:T(128)S(6)} %select_n.33), kind=kOutput, calls=%fused_computation.5 | convolution fusion | flops 536870912 | bytes 3670020 | tf_op jit(solution)/shard_map/dot_general | solution.py:28
  68.2 0.0 copy-done.5
  68.2 0.7 convolution_bitcast_fusion.1
  68.9 1.5 %pad_maximum_fusion = f32[256,2,4,256]{3,0,2,1:T(8,128)} fusion(f32[256,1,4,256]{3,0,2,1:T(8,128)S(1)} %convolution_bitcast_fusion.2, f32[256,1,4,256]{3,0,2,1:T(8,128)S(1)} %convolution_bitcast_fusion.1), kind=kLoop, calls=%fused_computation.3 | loop fusion | flops 524288 | bytes 4194304 | tf_op jit(solution)/shard_map/stack | solution.py:32
  70.4 0.0 copy-start.2
  70.4 0.0 copy-start.3
  70.4 0.0 copy-start.1
  70.4 0.0 reduce-scatter.2.cloned.1.call-update
  70.4 0.6 copy-done.2
  71.1 0.1 dynamic_slice.8
  71.2 0.0 copy-done.3
  71.2 0.0 copy-done.1
  71.2 0.6 gather_fusion.1
  71.8 0.6 fusion.16
  72.4 0.7 broadcast_add_fusion
  73.1 0.1 broadcast_subtract_fusion
  73.2 33.5 %reduce-scatter.2.cloned.1.call-done = f32[32,2,4,256]{3,0,2,1:T(8,128)} async-done(((f32[256,2,4,256]{3,0,2,1:T(8,128)}), f32[32,2,4,256]{3,0,2,1:T(8,128)}) %reduce-scatter.2.cloned.1.call-update) | async-done | bytes 262160 | tf_op jit(solution)/shard_map/reduce_scatter | solution.py:31
  106.7 1.0 bitcast_divide_fusion
  107.7 0.7 copy.34
  108.4 1.2 fusion.12
  109.6 15.1 %psum.7 = f32[1,4]{1,0:T(1,128)} all-reduce(f32[1,4]{1,0:T(1,128)S(1)} %bitcast.69), channel_id=1, replica_groups=mesh['aux'=4,'blk'=8] {'blk'}, use_global_device_ids=true, to_apply=%region_3.4 | all-reduce | flops 4 | bytes 32 | tf_op jit(solution)/shard_map/psum | solution.py:59
  (4 shorter events, 0.0 us)
Async XLA Ops:
  7.2 1.9 %copy-start = (bf16[6144,256]{1,0:T(8,128)(2,1)S(1)}, bf16[6144,256]{1,0:T(8,128)(2,1)}, u32[]{:S(2)}) copy-start(bf16[6144,256]{1,0:T(8,128)(2,1)} %param.12) | copy-start | bytes 9437188
  7.2 58.4 %all-gather.2.cloned.1.call-start = ((), (), s32[]{:S(2)}) async-start(), calls=%async_computation.1 | async-start | bytes 2621440 | tf_op jit(solution)/shard_map/all_gather | solution.py:25
  15.4 8.4 %copy-start.4 = (s32[12]{0:T(128)S(1)}, s32[12]{0:T(128)}, u32[]{:S(2)}) copy-start(s32[12]{0:T(128)} %param.10) | copy-start | bytes 148
  27.5 79.1 %reduce-scatter.2.cloned.1.call-start = ((), (), s32[]{:S(2)}) async-start(), calls=%async_computation.2 | async-start | bytes 2359296 | tf_op jit(solution)/shard_map/reduce_scatter | solution.py:31
  65.6 2.6 %copy-start.5 = (bf16[8,128,4,256]{3,1,2,0:T(8,128)(2,1)S(1)}, bf16[8,128,4,256]{3,1,2,0:T(8,128)(2,1)}, u32[]{:S(2)}) copy-start(bf16[8,128,4,256]{3,1,2,0:T(8,128)(2,1)} %all-gather.2.cloned.1.call-done) | copy-start | bytes 6291460
  70.4 0.7 copy-start.2
  70.4 0.8 copy-start.3
  70.4 0.8 copy-start.1
Sparse Core Ops, SparseCore 0:
  27.6 37.8 all-gather.1
  70.6 36.0 reduce-scatter.1
where the time goes:
time: 132 us; the launch traced here: 131 us
  waiting for transfers between devices  71.6 us (54%)
  blocking collectives  15.1 us (11%)
  between operations  14.8 us (11%)
  local copies, waits for them, and re-layouts  12.5 us (9%)
  matrix products  11 us (8%)
  other arithmetic  6.57 us (5%)
    all_gather x1, waiting for transfers between devices, body(): halfed = lax.all_gather(local_rows, 'aux', axis=0, tiled=True)  38 us
    reduce_scatter x1, waiting for transfers between devices, body(): lax.psum_scatter(jnp.stack([lax.dot_general(own_rows, halfed, (((0, 1), (...  33.5 us
    psum x1, blocking collectives, body(): pair_energy = lax.psum(pair_part, 'blk')[None]  15.1 us
    dot_general x1, local copies, waits for them, and re-layouts, body(): jnp.einsum('soqn,snv->soqv', three_center, coefficients, preferred_elemen...  7.69 us
    dot_general x1, matrix products, body(): jnp.einsum('soqn,snv->soqv', three_center, coefficients, preferred_elemen...  4.8 us
    dot_general x1, matrix products, body(): jnp.einsum('sk,soqv->kqov', select, products).astype(jnp.bfloat16)  2.88 us
  transfers between devices with their start and end apart: 2, of which 2 were waited for; matrix products, arithmetic and copies ran while one was open for 2% of the time, Pallas kernels for 0%

commit v1 on v0

--- a/solution.py
+++ b/solution.py
@@ -22,7 +22,12 @@
     select = (slot_aux[:, None] == jnp.arange(AUX_BLOCKS_DEV)[None, :]).astype(jnp.float32)
     select = select * keep[:, None]
     local_rows = jnp.einsum("sk,soqv->kqov", select, products).astype(jnp.bfloat16)
-    halfed = lax.all_gather(local_rows, "aux", axis=0, tiled=True)
+    ring = [local_rows]
+    for hop in range(3):
+        ring.append(lax.ppermute(ring[-1], "aux", [(dev, (dev + 1) % 4) for dev in range(4)]))
+    halfed = jnp.roll(
+        jnp.concatenate(ring[::-1], axis=0), (lax.axis_index("aux") + 1) * ring[0].shape[0], axis=0
+    )
     own_rows = lax.dynamic_index_in_dim(halfed, occ_row, 2, keepdims=False)
     rows_dev = vir_count // blk_count
     mixed = lax.dot_general(

time: 132 us -> 164 us (1.24); the launches traced: 131 us -> 162 us
  local copies, waits for them, and re-layouts: 12.5 us -> 38.6 us
  starting transfers between devices: 0.08 us -> 3.8 us
    ppermute x0 -> x3, waiting for transfers between devices: none -> 39.6 us  [body(): lax.ppermute(ring[-1], 'aux', [(dev, (dev + 1) % 4) for dev in range(4)])]
    all_gather x1 -> x0, waiting for transfers between devices: 38 us -> none  [body(): halfed = lax.all_gather(local_rows, 'aux', axis=0, tiled=True)]
    concatenate x0 -> x1, local copies, waits for them, and re-layouts: none -> 20 us  [body(): jnp.roll(jnp.concatenate(ring[::-1], axis=0), (lax.axis_index('aux') + 1)...]
    dynamic_slice x0 -> x3, local copies, waits for them, and re-layouts: none -> 4.34 us  [the longest x1 2.84 us: body(): jnp.roll(jnp.concatenate(ring[::-1], axis=0), (lax.axis_index('aux') + 1)...]
    ppermute x0 -> x3, starting transfers between devices: none -> 3.76 us  [body(): lax.ppermute(ring[-1], 'aux', [(dev, (dev + 1) % 4) for dev in range(4)])]
  transfers between devices with their start and end apart: 2 -> 4, of which waited for: 2 -> 4; matrix products, arithmetic and copies ran while one was open for 2% -> 1% of each run, Pallas kernels for 0% -> 0%
where the time goes in v1:
time: 164 us; the launch traced here: 162 us
  waiting for transfers between devices  72.9 us (44%)
  local copies, waits for them, and re-layouts  38.6 us (24%)
  blocking collectives  15.4 us (9%)
  between operations  14.8 us (9%)
  matrix products  9.58 us (6%)
  other arithmetic  6.56 us (4%)
  starting transfers between devices  3.8 us (2%)
    ppermute x3, waiting for transfers between devices, body(): lax.ppermute(ring[-1], 'aux', [(dev, (dev + 1) % 4) for dev in range(4)])  39.6 us
    reduce_scatter x1, waiting for transfers between devices, body(): lax.psum_scatter(jnp.stack([lax.dot_general(own_rows, halfed, (((0, 1), (...  33.2 us
    concatenate x1, local copies, waits for them, and re-layouts, body(): jnp.roll(jnp.concatenate(ring[::-1], axis=0), (lax.axis_index('aux') + 1)...  20 us
    psum x1, blocking collectives, body(): pair_energy = lax.psum(pair_part, 'blk')[None]  15.4 us
    dot_general x1, local copies, waits for them, and re-layouts, body(): jnp.einsum('soqn,snv->soqv', three_center, coefficients, preferred_elemen...  7.71 us
    dot_general x1, matrix products, body(): jnp.einsum('soqn,snv->soqv', three_center, coefficients, preferred_elemen...  4.81 us
    ppermute x3, starting transfers between devices, body(): lax.ppermute(ring[-1], 'aux', [(dev, (dev + 1) % 4) for dev in range(4)])  3.76 us
  transfers between devices with their start and end apart: 4, of which 4 were waited for; matrix products, arithmetic and copies ran while one was open for 1% of the time, Pallas kernels for 0%

profile of v1, /device:TPU:0, one launch (start us, length us, event | category | flops | bytes accessed | tf_op | source)
XLA Modules:
  0.0 161.6 jit_solution(11357698906469877163)
XLA Ops:
  7.2 0.0 copy-start
  7.2 0.0 reduce-scatter.2.cloned.1.call-start
  7.2 0.8 compare_and_fusion
  8.0 0.8 compare_select_fusion.1
  9.5 0.0 copy-done
  9.5 1.5 gather_fusion
  11.0 4.8 %fusion.13 = bf16[12,256,4,128]{3,1,2,0:T(8,128)(2,1)} fusion(bf16[12,4,128,128]{3,2,1,0:T(8,128)(2,1)} %param.8, bf16[12,128,256]{2,1,0:T(8,128)(2,1)} %gather_fusion, pred[12]{0:T(512)(128)(4,1)S(1)} %compare_and_fusion), kind=kOutput, calls=%fused_computation.11 | convolution fusion | flops 403046400 | bytes 5505036 | tf_op jit(solution)/shard_map/soqn,snv->soqv/dot_general | solution.py:18
  15.8 0.0 copy-start.6
  15.8 7.7 %copy.20 = bf16[12,256,4,128]{1,0,3,2:T(8,128)(2,1)} copy(bf16[12,256,4,128]{3,1,2,0:T(8,128)(2,1)} %fusion.13) | data formatting | bytes 6291456 | tf_op jit(solution)/shard_map/soqn,snv->soqv/dot_general | solution.py:18
  23.5 0.0 copy-done.6
  23.5 2.9 %fusion.10 = bf16[2,128,4,256]{3,0,1,2:T(2,128)(2,1)S(1)} fusion(bf16[12,256,4,128]{1,0,3,2:T(8,128)(2,1)} %copy.20, bf16[12]{0:T(256)(128)(2,1)S(1)} %compare_convert_fusion, s32[12]{0:T(128)S(1)} %copy-done.6), kind=kOutput, calls=%fused_computation.10 | convolution fusion | flops 6291504 | bytes 3670088 | tf_op jit(solution)/shard_map/sk,soqv->kqov/dot_general | solution.py:24
  26.4 0.0 copy-start.2
  26.4 0.8 copy-done.2
  27.2 3.0 %collective-permute-start = (bf16[2,128,4,256]{3,0,1,2:T(2,128)(2,1)S(1)}, bf16[2,128,4,256]{3,0,1,2:T(2,128)(2,1)S(1)}, u32[]{:S(2)}, u32[]{:S(2)}) collective-permute-start(bf16[2,128,4,256]{3,0,1,2:T(2,128)(2,1)S(1)} %fusion.10), channel_id=1, source_target_pairs={{0,8},{8,16},{16,24},{24,0},{1,9},{9,17},{17,25},{25,1},{2,10},{10... | collective-permute-start | bytes 1572872 | tf_op jit(solution)/shard_map/ppermute | solution.py:27
  30.2 12.9 %collective-permute-done = bf16[2,128,4,256]{3,0,1,2:T(2,128)(2,1)S(1)} collective-permute-done((bf16[2,128,4,256]{3,0,1,2:T(2,128)(2,1)S(1)}, bf16[2,128,4,256]{3,0,1,2:T(2,128)(2,1)S(1)}, u32[]{:S(2)}, u32[]{:S(2)}) %collective-permute-start) | collective-permute-done | bytes 524320 | tf_op jit(solution)/shard_map/ppermute | solution.py:27
  43.0 0.0 copy-start.3
  43.0 0.8 copy-done.3
  43.8 0.8 collective-permute-start.1
  44.6 13.3 %collective-permute-done.1 = bf16[2,128,4,256]{3,0,1,2:T(2,128)(2,1)} collective-permute-done((bf16[2,128,4,256]{3,0,1,2:T(2,128)(2,1)S(1)}, bf16[2,128,4,256]{3,0,1,2:T(2,128)(2,1)}, u32[]{:S(2)}, u32[]{:S(2)}) %collective-permute-start.1) | collective-permute-done | bytes 524320 | tf_op jit(solution)/shard_map/ppermute | solution.py:27
  57.9 0.0 collective-permute-start.2
  57.9 13.4 %collective-permute-done.2 = bf16[2,128,4,256]{3,0,1,2:T(2,128)(2,1)} collective-permute-done((bf16[2,128,4,256]{3,0,1,2:T(2,128)(2,1)}, bf16[2,128,4,256]{3,0,1,2:T(2,128)(2,1)}, u32[]{:S(2)}, u32[]{:S(2)}) %collective-permute-start.2) | collective-permute-done | bytes 524320 | tf_op jit(solution)/shard_map/ppermute | solution.py:27
  71.4 20.0 %concatenate.6 = bf16[16,128,4,256]{3,0,1,2:T(8,128)(2,1)} concatenate(bf16[2,128,4,256]{3,0,1,2:T(2,128)(2,1)} %collective-permute-done.2, bf16[2,128,4,256]{3,0,1,2:T(2,128)(2,1)} %collective-permute-done.1, bf16[2,128,4,256]{3,0,1,2:T(2,128)(2,1)} %copy-done.3, bf16[2,128,4,256]{3,0,1,2:T(2,128)(2,1)} %copy-done.2, bf16[2,128,4,256]{3,0,1,2:T(2,128)(2,1)} %collective-permute-done.2, ...), dimensions={0} | concatenate | bytes 8388608 | tf_op jit(solution)/shard_map/jit(_roll_dynamic)/concatenate | solution.py:28
  91.4 1.4 fusion.35
  92.7 1.4 constant_dynamic-slice_fusion.1
  94.1 2.8 %constant_dynamic-slice_fusion = bf16[8,128,4,256]{3,0,1,2:T(8,128)(2,1)S(1)} fusion(bf16[16,128,4,256]{3,0,1,2:T(8,128)(2,1)} %concatenate.6, s32[]{:T(128)S(6)} %select_n.51), kind=kLoop, calls=%fused_computation.42 | loop fusion | bytes 4194308 | tf_op jit(solution)/shard_map/jit(_roll_dynamic)/dynamic_slice | solution.py:28
  97.0 0.1 copy.39
  97.1 1.1 convolution_bitcast_fusion
  98.2 0.8 fusion.4
  99.0 1.5 pad_maximum_fusion
  100.5 0.0 copy-start.4
  100.5 0.0 copy-start.5
  100.5 0.0 copy-start.1
  100.5 0.0 reduce-scatter.2.cloned.1.call-update
  100.5 0.6 copy-done.4
  101.2 0.1 dynamic_slice.14
  101.2 0.0 copy-done.5
  101.3 0.0 copy-done.1
  101.3 0.6 gather_fusion.1
  101.9 0.6 fusion.27
  102.5 0.7 broadcast_add_fusion
  103.2 0.1 broadcast_subtract_fusion
  103.2 33.2 %reduce-scatter.2.cloned.1.call-done = f32[32,2,4,256]{3,0,2,1:T(8,128)} async-done(((f32[256,2,4,256]{3,0,2,1:T(8,128)}), f32[32,2,4,256]{3,0,2,1:T(8,128)}) %reduce-scatter.2.cloned.1.call-update) | async-done | bytes 262160 | tf_op jit(solution)/shard_map/reduce_scatter | solution.py:36
  136.5 1.0 bitcast_divide_fusion
  137.5 0.7 copy.18
  138.2 1.2 fusion.23
  139.4 15.4 %psum.7 = f32[1,4]{1,0:T(1,128)} all-reduce(f32[1,4]{1,0:T(1,128)S(1)} %bitcast.65), channel_id=1, replica_groups=mesh['aux'=4,'blk'=8] {'blk'}, use_global_device_ids=true, to_apply=%region_3.4 | all-reduce | flops 4 | bytes 32 | tf_op jit(solution)/shard_map/psum | solution.py:64
  (4 shorter events, 0.0 us)
Async XLA Ops:
  7.2 2.3 %copy-start = (bf16[6144,256]{1,0:T(8,128)(2,1)S(1)}, bf16[6144,256]{1,0:T(8,128)(2,1)}, u32[]{:S(2)}) copy-start(bf16[6144,256]{1,0:T(8,128)(2,1)} %param.12) | copy-start | bytes 9437188
  7.2 129.3 %reduce-scatter.2.cloned.1.call-start = ((), (), s32[]{:S(2)}) async-start(), calls=%async_computation.1 | async-start | bytes 2359296 | tf_op jit(solution)/shard_map/reduce_scatter | solution.py:36
  15.8 7.7 %copy-start.6 = (s32[12]{0:T(128)S(1)}, s32[12]{0:T(128)}, u32[]{:S(2)}) copy-start(s32[12]{0:T(128)} %param.10) | copy-start | bytes 148
  26.4 0.8 copy-start.2
  27.2 15.8 %collective-permute-start = (bf16[2,128,4,256]{3,0,1,2:T(2,128)(2,1)S(1)}, bf16[2,128,4,256]{3,0,1,2:T(2,128)(2,1)S(1)}, u32[]{:S(2)}, u32[]{:S(2)}) collective-permute-start(bf16[2,128,4,256]{3,0,1,2:T(2,128)(2,1)S(1)} %fusion.10), channel_id=1, source_target_pairs={{0,8},{8,16},{16,24},{24,0},{1,9},{9,17},{17,25},{25,1},{2,10},{10... | collective-permute-start | bytes 1572872 | tf_op jit(solution)/shard_map/ppermute | solution.py:27
  43.0 0.8 copy-start.3
  43.8 14.1 %collective-permute-start.1 = (bf16[2,128,4,256]{3,0,1,2:T(2,128)(2,1)S(1)}, bf16[2,128,4,256]{3,0,1,2:T(2,128)(2,1)}, u32[]{:S(2)}, u32[]{:S(2)}) collective-permute-start(bf16[2,128,4,256]{3,0,1,2:T(2,128)(2,1)S(1)} %collective-permute-done), channel_id=1, source_target_pairs={{0,8},{8,16},{16,24},{24,0},{1,9},{9,17},{17,25},{25,1},{2,10},{10... | collective-permute-start | bytes 1572872 | tf_op jit(solution)/shard_map/ppermute | solution.py:27
  57.9 13.4 %collective-permute-start.2 = (bf16[2,128,4,256]{3,0,1,2:T(2,128)(2,1)}, bf16[2,128,4,256]{3,0,1,2:T(2,128)(2,1)}, u32[]{:S(2)}, u32[]{:S(2)}) collective-permute-start(bf16[2,128,4,256]{3,0,1,2:T(2,128)(2,1)} %collective-permute-done.1), channel_id=1, source_target_pairs={{0,8},{8,16},{16,24},{24,0},{1,9},{9,17},{17,25},{25,1},{2,10},{10... | collective-permute-start | bytes 1572872 | tf_op jit(solution)/shard_map/ppermute | solution.py:27
  100.5 0.7 copy-start.4
  100.5 0.8 copy-start.5
  100.5 0.8 copy-start.1
Sparse Core Ops, SparseCore 0:
  100.6 35.7 reduce-scatter.1
